TPU v7x, 128 devices: a whole 4x4x4 slice. The times are simulated.
128 devices in a mesh: pair: 16 (over y_hi, z, core), rows: 8 (over y_lo, x).
Axes of the slice: x: 4, y: 4 (y_hi: 2, y_lo: 2; y = y_hi * 2 + y_lo), z: 4, core: 2. Of those that a mesh axis runs over, the one named last changes fastest.
Arguments:
- matrix: float32 [4096, 16384], P(('rows', 'pair')), may hold values from -6 to 6
- plan: int32 [32], replicated, may hold values from 0 to 31, each once
Outputs:
- rotated: float32 [4096, 16384], P('rows', 'pair')
Inputs may be any that keep to these rules, and one draw needn't show every extreme that they name: `plan`: each block number appears once.
All inputs are finite; a program needn't handle non-finite values.
Results may differ from a plain program's by a relative error of at most 0.0003.
Values sent between devices are 32-bit elements; how exact they have to be, the bound alone decides.
A program may use at most 64 MiB of HBM per device.

v0:
```python
import jax
import jax.numpy as jnp
from jax import lax
from jax.sharding import PartitionSpec as P

BLK = 512
STEPS = 2


epsilon = 1e-06
high = lax.Precision.HIGHEST


def from_behind(x, axis, by):
    count = lax.axis_size(axis)
    pairs = [(i, i + by) for i in range(count) if 0 <= i + by < count]
    return lax.ppermute(x, axis, pairs)


def inner_gram(left, right):
    return lax.dot_general(
        left, right, (((0,), (0,)), ((), ())), precision=high, preferred_element_type=jnp.float32
    )


def normalize(gram):
    width = gram.shape[0]
    diagonal = jnp.diagonal(gram) + epsilon
    inverse = 1.0 / jnp.sqrt(diagonal)
    normed = gram * inverse[:, None] * inverse[None, :]
    spread = 1.5 * jnp.sqrt(jnp.sum(normed * normed)) / jnp.sqrt(jnp.float32(width))
    scaled_gram = normed / spread
    identity = jnp.eye(width, dtype=jnp.float32)
    first_iter = 0.5 * (3.0 * identity - scaled_gram)
    factor = 0.5 * jnp.sqrt(diagonal) / jnp.sqrt(spread)
    return (scaled_gram, first_iter, inverse, factor, identity)


def per_device(matrix, plan):
    local_rows = matrix.shape[0]
    blocks = matrix.reshape(local_rows, -1, BLK)
    slots = jnp.take(blocks, plan, axis=1).reshape(local_rows, -1)
    current = lax.all_to_all(slots, "pair", split_axis=1, concat_axis=0, tiled=True)
    pair_index = lax.axis_index("pair")
    pair_count = lax.axis_size("pair")
    for turn_index in range(STEPS):
        upper = current[:, :BLK]
        lower = current[:, BLK:]
        upper_gram, lower_gram, cross_gram = lax.psum(
            (inner_gram(upper, upper), inner_gram(lower, lower), inner_gram(upper, lower)), "rows"
        )
        gram = jnp.concatenate(
            [
                jnp.concatenate([upper_gram, cross_gram], axis=1),
                jnp.concatenate([cross_gram.T, lower_gram], axis=1),
            ],
            axis=0,
        )
        scaled_gram, first_iter, inverse, factor, identity = normalize(gram)
        weighted = current * inverse[None, :]
        second_term = jnp.dot(
            scaled_gram, first_iter, precision=high, preferred_element_type=jnp.float32
        )
        middle = 3.0 * identity - jnp.dot(
            first_iter, second_term, precision=high, preferred_element_type=jnp.float32
        )
        product = jnp.dot(weighted, middle, precision=high, preferred_element_type=jnp.float32)
        current = (
            jnp.dot(product, first_iter, precision=high, preferred_element_type=jnp.float32)
            * factor[None, :]
        )
        upper = current[:, :BLK]
        lower = current[:, BLK:]
        outgoing = jnp.where(pair_index == 0, lower, upper)
        arrived_up = from_behind(outgoing, "pair", 1)
        arrived_down = from_behind(lower, "pair", -1)
        new_upper = jnp.where(pair_index == 0, upper, arrived_up)
        new_lower = jnp.where(pair_index == pair_count - 1, upper, arrived_down)
        current = jnp.concatenate([new_upper, new_lower], axis=1)
    return current


def solution(mesh):
    placed = (P(("rows", "pair"), None), P())
    return jax.shard_map(
        per_device, mesh=mesh, in_specs=placed, out_specs=P("rows", "pair"), check_vma=False
    )
```

profile of v0, /device:TPU:97, one launch (start us, length us, event | category | flops | bytes accessed | tf_op | source)
XLA Modules:
  0.0 464.6 jit_solution(5167096289659873368)
XLA Ops:
  6.5 0.7 compare_select_fusion
  7.2 0.7 compare_and_fusion
  7.9 1.8 copy.35
  9.7 2.0 gather_fusion
  11.7 4.1 copy.22
  15.8 1.9 gather.14
  18.3 1.2 copy.23
  19.5 34.5 %all_to_all.16 = f32[32,16,1024]{2,0,1:T(8,128)S(1)} all-to-all(f32[32,16,1024]{2,0,1:T(8,128)S(1)} %copy.23), channel_id=1, replica_groups=mesh['pair'=16,'rows'=8] {'pair'}, dimensions={1} | all-to-all | bytes 4194304 | tf_op jit(solution)/shard_map/all_to_all | solution.py:43
  54.0 2.9 fusion.51
  56.9 2.9 fusion.53
  59.8 2.9 fusion.56
  62.7 0.3 all-reduce.5.cloned.1.call-start
  63.0 87.6 %all-reduce.7.cloned.1.call-done = (f32[512,512]{1,0:T(8,128)}, f32[512,512]{0,1:T(8,128)}, f32[512,512]{1,0:T(8,128)}) async-done(((f32[512,512]{1,0:T(8,128)}, f32[512,512]{0,1:T(8,128)}, f32[512,512]{1,0:T(8,128)}), (f32[512,512]{1,0:T(8,128)}, f32[512,512]{0,1:T(8,128)}, f32[512,512]{1,0:T(8,128)})) %all-reduce.7.cloned.1.call-update) | async-done | bytes 3145744 | tf_op jit(solution)/shard_map/psum | solution.py:49
  150.6 1.6 copy.25
  152.2 1.0 copy-done.3
  153.1 4.3 maximum_maximum_fusion
  157.5 16.9 %gather_fusion.1 = f32[1024]{0:T(1024)S(1)} fusion(f32[1024,1024]{1,0:T(8,128)} %maximum_maximum_fusion, s32[1024]{0:T(1024)S(1)} %bitcast.23), kind=kCustom, calls=%fused_computation.1 | custom fusion | bytes 16384 | tf_op jit(solution)/shard_map/jit(diagonal)/cond/branch_0_fun/gather | solution.py:28
  174.4 3.7 multiply_reduce_fusion.1
  178.9 20.5 %fusion.14 = f32[1024,1024]{1,0:T(8,128)S(1)} fusion(f32[]{:T(128)S(6)} %div.44, f32[1024]{0:T(1024)S(1)} %add_rsqrt_fusion.1, f32[512,512]{1,0:T(8,128)} %get-tuple-element.8, f32[512,512]{1,0:T(8,128)S(1)} %bitcast.31, f32[512,512]{1,0:T(8,128)} %copy-done.3, f32[512,512]{1,0:T(8,128)} %get-tuple-element.10), kind=kOutput, calls=%fused_computation.23 | convolution fusion | flops 12901679104 | bytes 8392708 | tf_op jit(solution)/shard_map/dot_general | solution.py:61
  199.5 14.2 %fusion.12 = f32[1024,1024]{1,0:T(8,128)S(1)} fusion(f32[1024,1024]{1,0:T(8,128)S(1)} %fusion.14, f32[]{:T(128)S(6)} %div.44, f32[1024]{0:T(1024)S(1)} %add_rsqrt_fusion.1, f32[512,512]{1,0:T(8,128)S(1)} %copy-done.7, f32[512,512]{1,0:T(8,128)S(1)} %bitcast.32, f32[512,512]{1,0:T(8,128)S(1)} %copy-done.4, f32[512,512]{1,0:T(8,128)S(1)} %copy-done.8), kind=kOutput, calls=%fused_computation.22 | convolution fusion | flops 12895387648 | bytes 12587012 | tf_op jit(solution)/shard_map/dot_general | solution.py:64
  213.6 6.9 %fusion.1 = f32[512,1024]{1,0:T(8,128)S(1)} fusion(f32[1024,1024]{1,0:T(8,128)S(1)} %fusion.12, f32[512,1024]{1,0:T(8,128)S(1)} %bitcast.28, f32[1024]{0:T(1024)S(1)} %add_rsqrt_fusion.1), kind=kOutput, calls=%fused_computation.8 | convolution fusion | flops 6446120960 | bytes 8392704 | tf_op jit(solution)/shard_map/dot_general | solution.py:67
  220.6 7.7 %fusion.43 = f32[512,1024]{1,0:T(8,128)S(1)} fusion(f32[512,1024]{1,0:T(8,128)S(1)} %fusion.1, f32[1024]{0:T(1024)S(1)} %multiply_divide_fusion.1, f32[]{:T(128)S(6)} %div.44, f32[1024]{0:T(1024)S(1)} %add_rsqrt_fusion.1, f32[512,512]{1,0:T(8,128)S(1)} %copy-done.7, f32[512,512]{1,0:T(8,128)S(1)} %bitcast.33, f32[512,512]{1,0:T(8,128)S(1)} %copy-done.4, ...), kind=kOutput, calls=%fused_computation.55 | convolution fusion | flops 6453460992 | bytes 8396804 | tf_op jit(solution)/shard_map/dot_general | solution.py:69
  228.3 1.4 slice_select_fusion.5
  229.7 6.1 %collective-permute-start = (f32[512,512]{1,0:T(8,128)}, f32[512,512]{1,0:T(8,128)}, u32[]{:S(2)}, u32[]{:S(2)}) collective-permute-start(f32[512,512]{1,0:T(8,128)} %get-tuple-element.17), channel_id=1, source_target_pairs={{0,8},{8,16},{16,24},{24,32},{32,40},{40,48},{48,56},{56,64},{64,7... | collective-permute-start | bytes 3145736 | tf_op jit(solution)/shard_map/ppermute | solution.py:17
  235.8 1.9 collective-permute-start.1
  237.7 10.1 %collective-permute-done = f32[512,512]{1,0:T(8,128)} collective-permute-done((f32[512,512]{1,0:T(8,128)}, f32[512,512]{1,0:T(8,128)}, u32[]{:S(2)}, u32[]{:S(2)}) %collective-permute-start) | collective-permute-done | bytes 1048608 | tf_op jit(solution)/shard_map/ppermute | solution.py:17
  247.8 7.8 %collective-permute-done.1 = f32[512,512]{1,0:T(8,128)} collective-permute-done((f32[512,512]{1,0:T(8,128)S(1)}, f32[512,512]{1,0:T(8,128)}, u32[]{:S(2)}, u32[]{:S(2)}) %collective-permute-start.1) | collective-permute-done | bytes 1048608 | tf_op jit(solution)/shard_map/ppermute | solution.py:17
  255.6 2.2 slice_select_fusion.4
  257.9 2.9 fusion.87
  260.8 2.9 fusion.88
  263.7 2.9 fusion.89
  266.6 86.5 %all-reduce.5.cloned.1.call-done = (f32[512,512]{1,0:T(8,128)}, f32[512,512]{0,1:T(8,128)}, f32[512,512]{0,1:T(8,128)}) async-done(((f32[512,512]{1,0:T(8,128)}, f32[512,512]{0,1:T(8,128)}, f32[512,512]{0,1:T(8,128)}), (f32[512,512]{1,0:T(8,128)}, f32[512,512]{0,1:T(8,128)}, f32[512,512]{0,1:T(8,128)})) %all-reduce.5.cloned.1.call-update) | async-done | bytes 3145744 | tf_op jit(solution)/shard_map/psum | solution.py:49
  353.1 3.0 pad_maximum_fusion
  356.1 1.9 copy.28
  358.1 4.0 maximum_maximum_fusion.1
  362.1 17.3 %gather_fusion.2 = f32[1024]{0:T(1024)S(1)} fusion(f32[1024,1024]{1,0:T(8,128)} %maximum_maximum_fusion.1, s32[1024]{0:T(1024)S(1)} %bitcast.24), kind=kCustom, calls=%fused_computation.2 | custom fusion | bytes 16384 | tf_op jit(solution)/shard_map/jit(diagonal)/cond/branch_0_fun/gather | solution.py:28
  379.4 3.4 multiply_reduce_fusion
  383.5 16.9 %fusion.8 = f32[1024,1024]{1,0:T(8,128)S(1)} fusion(f32[]{:T(128)S(6)} %div.49, f32[1024]{0:T(1024)S(1)} %add_rsqrt_fusion, f32[512,512]{1,0:T(8,128)} %get-tuple-element.5, f32[512,512]{1,0:T(8,128)} %bitcast.36, f32[512,1024]{1,0:T(8,128)S(1)} %copy.28), kind=kOutput, calls=%fused_computation.20 | convolution fusion | flops 12899581952 | bytes 8392708 | tf_op jit(solution)/shard_map/dot_general | solution.py:61
  400.5 14.2 %fusion.6 = f32[1024,1024]{1,0:T(8,128)S(1)} fusion(f32[1024,1024]{1,0:T(8,128)S(1)} %fusion.8, f32[]{:T(128)S(6)} %div.49, f32[1024]{0:T(1024)S(1)} %add_rsqrt_fusion, f32[512,512]{1,0:T(8,128)S(1)} %copy-done.9, f32[512,512]{1,0:T(8,128)S(1)} %bitcast.37, f32[512,1024]{1,0:T(8,128)S(1)} %copy.28), kind=kOutput, calls=%fused_computation.19 | convolution fusion | flops 12894339072 | bytes 12587012 | tf_op jit(solution)/shard_map/dot_general | solution.py:64
  414.7 6.9 %fusion.3 = f32[512,1024]{1,0:T(8,128)S(1)} fusion(f32[1024,1024]{1,0:T(8,128)S(1)} %fusion.6, f32[512,512]{1,0:T(8,128)S(1)} %copy-done.1, f32[512,512]{1,0:T(8,128)S(1)} %get-tuple-element.15, f32[1024]{0:T(1024)S(1)} %add_rsqrt_fusion), kind=kOutput, calls=%fused_computation.10 | convolution fusion | flops 6446645248 | bytes 8392704 | tf_op jit(solution)/shard_map/dot_general | solution.py:67
  421.6 7.8 %fusion.46 = f32[512,1024]{1,0:T(8,128)S(1)} fusion(f32[512,1024]{1,0:T(8,128)S(1)} %fusion.3, f32[1024]{0:T(1024)S(1)} %multiply_divide_fusion, f32[]{:T(128)S(6)} %div.49, f32[1024]{0:T(1024)S(1)} %add_rsqrt_fusion, f32[512,512]{1,0:T(8,128)S(1)} %copy-done.9, f32[512,512]{1,0:T(8,128)S(1)} %bitcast.38, f32[512,1024]{1,0:T(8,128)S(1)} %copy.28), kind=kOutput, calls=%fused_computation.56 | convolution fusion | flops 6452412416 | bytes 8396804 | tf_op jit(solution)/shard_map/dot_general | solution.py:69
  429.4 0.2 slice_select_fusion.2
  429.6 6.1 %collective-permute-start.2 = (f32[512,512]{1,0:T(8,128)S(1)}, f32[512,512]{1,0:T(8,128)S(1)}, u32[]{:S(2)}, u32[]{:S(2)}) collective-permute-start(f32[512,512]{1,0:T(8,128)S(1)} %get-tuple-element.13), channel_id=1, source_target_pairs={{0,8},{8,16},{16,24},{24,32},{32,40},{40,48},{48,56},{56,64},{64,7... | collective-permute-start | bytes 3145736 | tf_op jit(solution)/shard_map/ppermute | solution.py:17
  435.7 1.9 collective-permute-start.3
  437.7 9.8 %collective-permute-done.2 = f32[512,512]{1,0:T(8,128)S(1)} collective-permute-done((f32[512,512]{1,0:T(8,128)S(1)}, f32[512,512]{1,0:T(8,128)S(1)}, u32[]{:S(2)}, u32[]{:S(2)}) %collective-permute-start.2) | collective-permute-done | bytes 1048608 | tf_op jit(solution)/shard_map/ppermute | solution.py:17
  447.5 8.0 %collective-permute-done.3 = f32[512,512]{1,0:T(8,128)S(1)} collective-permute-done((f32[512,512]{1,0:T(8,128)S(1)}, f32[512,512]{1,0:T(8,128)S(1)}, u32[]{:S(2)}, u32[]{:S(2)}) %collective-permute-start.3) | collective-permute-done | bytes 1048608 | tf_op jit(solution)/shard_map/ppermute | solution.py:17
  455.5 0.3 slice_select_fusion.1
  455.8 1.5 pad_maximum_fusion.1
  (32 shorter events, 0.6 us)
Async XLA Ops:
  6.5 144.1 %all-reduce.7.cloned.1.call-start = ((), (), s32[]{:S(2)}) async-start(), calls=%async_computation.2 | async-start | bytes 6291456 | tf_op jit(solution)/shard_map/psum | solution.py:49
  62.7 290.4 %all-reduce.5.cloned.1.call-start = ((), (), s32[]{:S(2)}) async-start(), calls=%async_computation.1 | async-start | bytes 6291456 | tf_op jit(solution)/shard_map/psum | solution.py:49
  152.2 1.0 copy-start.3
  157.5 16.9 %copy-start.2 = (f32[512,512]{0,1:T(8,128)S(1)}, f32[512,512]{0,1:T(8,128)}, u32[]{:S(2)}) copy-start(f32[512,512]{0,1:T(8,128)} %get-tuple-element.9) | copy-start | bytes 3145732
  178.8 20.6 %copy-start.4 = (f32[512,512]{1,0:T(8,128)S(1)}, f32[512,512]{1,0:T(8,128)}, u32[]{:S(2)}) copy-start(f32[512,512]{1,0:T(8,128)} %copy-done.3) | copy-start | bytes 3145732
  178.8 20.6 %copy-start.7 = (f32[512,512]{1,0:T(8,128)S(1)}, f32[512,512]{1,0:T(8,128)}, u32[]{:S(2)}) copy-start(f32[512,512]{1,0:T(8,128)} %get-tuple-element.8) | copy-start | bytes 3145732
  178.8 20.6 %copy-start.8 = (f32[512,512]{1,0:T(8,128)S(1)}, f32[512,512]{1,0:T(8,128)}, u32[]{:S(2)}) copy-start(f32[512,512]{1,0:T(8,128)} %get-tuple-element.10) | copy-start | bytes 3145732
  228.3 19.5 %copy-start.6 = (f32[512,1024]{1,0:T(8,128)}, f32[512,1024]{1,0:T(8,128)S(1)}, u32[]{:S(2)}) copy-start(f32[512,1024]{1,0:T(8,128)S(1)} %fusion.43) | copy-start | bytes 6291460
  229.7 18.1 %collective-permute-start = (f32[512,512]{1,0:T(8,128)}, f32[512,512]{1,0:T(8,128)}, u32[]{:S(2)}, u32[]{:S(2)}) collective-permute-start(f32[512,512]{1,0:T(8,128)} %get-tuple-element.17), channel_id=1, source_target_pairs={{0,8},{8,16},{16,24},{24,32},{32,40},{40,48},{48,56},{56,64},{64,7... | collective-permute-start | bytes 3145736 | tf_op jit(solution)/shard_map/ppermute | solution.py:17
  235.8 19.8 %collective-permute-start.1 = (f32[512,512]{1,0:T(8,128)S(1)}, f32[512,512]{1,0:T(8,128)}, u32[]{:S(2)}, u32[]{:S(2)}) collective-permute-start(f32[512,512]{1,0:T(8,128)S(1)} %get-tuple-element.18), channel_id=1, source_target_pairs={{8,0},{16,8},{24,16},{32,24},{40,32},{48,40},{56,48},{64,56},{72,6... | collective-permute-start | bytes 3145736 | tf_op jit(solution)/shard_map/ppermute | solution.py:17
  257.8 8.7 %copy-start = (f32[512,512]{1,0:T(8,128)}, f32[512,512]{1,0:T(8,128)S(1)}, u32[]{:S(2)}) copy-start(f32[512,512]{1,0:T(8,128)S(1)} %get-tuple-element.16) | copy-start | bytes 3145732
  383.5 16.9 %copy-start.5 = (f32[512,512]{0,1:T(8,128)S(1)}, f32[512,512]{0,1:T(8,128)}, u32[]{:S(2)}) copy-start(f32[512,512]{0,1:T(8,128)} %get-tuple-element.6) | copy-start | bytes 3145732
  383.5 16.9 %copy-start.9 = (f32[512,512]{1,0:T(8,128)S(1)}, f32[512,512]{1,0:T(8,128)}, u32[]{:S(2)}) copy-start(f32[512,512]{1,0:T(8,128)} %get-tuple-element.5) | copy-start | bytes 3145732
  400.5 14.2 %copy-start.1 = (f32[512,512]{1,0:T(8,128)S(1)}, f32[512,512]{1,0:T(8,128)}, u32[]{:S(2)}) copy-start(f32[512,512]{1,0:T(8,128)} %copy-done) | copy-start | bytes 3145732
  429.6 17.9 %collective-permute-start.2 = (f32[512,512]{1,0:T(8,128)S(1)}, f32[512,512]{1,0:T(8,128)S(1)}, u32[]{:S(2)}, u32[]{:S(2)}) collective-permute-start(f32[512,512]{1,0:T(8,128)S(1)} %get-tuple-element.13), channel_id=1, source_target_pairs={{0,8},{8,16},{16,24},{24,32},{32,40},{40,48},{48,56},{56,64},{64,7... | collective-permute-start | bytes 3145736 | tf_op jit(solution)/shard_map/ppermute | solution.py:17
  435.7 19.7 %collective-permute-start.3 = (f32[512,512]{1,0:T(8,128)S(1)}, f32[512,512]{1,0:T(8,128)S(1)}, u32[]{:S(2)}, u32[]{:S(2)}) collective-permute-start(f32[512,512]{1,0:T(8,128)S(1)} %get-tuple-element.14), channel_id=1, source_target_pairs={{8,0},{16,8},{24,16},{32,24},{40,32},{48,40},{56,48},{64,56},{72,6... | collective-permute-start | bytes 3145736 | tf_op jit(solution)/shard_map/ppermute | solution.py:17
Sparse Core Ops, SparseCore 0:
  62.8 87.7 all-reduce.6
  266.7 86.3 all-reduce.4
where the time goes:
time: 473 us; the launch traced here: 465 us
  waiting for transfers between devices  210 us (44%)
  matrix products  113 us (24%)
  local copies, waits for them, and re-layouts  50 us (11%)
  blocking collectives  34.5 us (7%)
  other arithmetic  25.7 us (5%)
  starting transfers between devices  16.3 us (3%)
  between operations  15.7 us (3%)
    psum x2, waiting for transfers between devices, per_device(): lax.psum((inner_gram(upper, upper), inner_gram(lower, lower), inner_gram(...  174 us
    dot_general x2, matrix products, per_device(): jnp.dot(scaled_gram, first_iter, precision=high, preferred_element_type=j...  37.4 us
    ppermute x4, waiting for transfers between devices, from_behind(): return lax.ppermute(x, axis, pairs)  35.7 us
    all_to_all x1, blocking collectives, per_device(): lax.all_to_all(slots, 'pair', split_axis=1, concat_axis=0, tiled=True)  34.5 us
    gather x2, local copies, waits for them, and re-layouts, normalize(): diagonal = jnp.diagonal(gram) + epsilon  34.2 us
    dot_general x2, matrix products, per_device(): jnp.dot(first_iter, second_term, precision=high, preferred_element_type=j...  28.4 us
    dot_general x6, matrix products, inner_gram(): lax.dot_general(left, right, (((0,), (0,)), ((), ())), precision=high, pr...  17.5 us
    ppermute x4, starting transfers between devices, from_behind(): return lax.ppermute(x, axis, pairs)  16.1 us
  transfers between devices with their start and end apart: 6, of which 6 were waited for; matrix products, arithmetic and copies ran while one was open for 0% of the time, Pallas kernels for 0%

commit v1 on v0

--- a/solution.py
+++ b/solution.py
@@ -9,6 +9,7 @@
 
 epsilon = 1e-06
 high = lax.Precision.HIGHEST
+fast = lax.Precision.HIGH
 
 
 def from_behind(x, axis, by):
@@ -23,9 +24,15 @@
     )
 
 
-def normalize(gram):
+def masked_diagonal(block):
+    width = block.shape[0]
+    eye = lax.broadcasted_iota(jnp.int32, (width, width), 0) == lax.broadcasted_iota(jnp.int32, (width, width), 1)
+    return jnp.sum(jnp.where(eye, block, 0.0), axis=0)
+
+
+def normalize(gram, diagonal):
     width = gram.shape[0]
-    diagonal = jnp.diagonal(gram) + epsilon
+    diagonal = diagonal + epsilon
     inverse = 1.0 / jnp.sqrt(diagonal)
     normed = gram * inverse[:, None] * inverse[None, :]
     spread = 1.5 * jnp.sqrt(jnp.sum(normed * normed)) / jnp.sqrt(jnp.float32(width))
@@ -56,17 +63,18 @@
             ],
             axis=0,
         )
-        scaled_gram, first_iter, inverse, factor, identity = normalize(gram)
+        diagonal = jnp.concatenate([masked_diagonal(upper_gram), masked_diagonal(lower_gram)])
+        scaled_gram, first_iter, inverse, factor, identity = normalize(gram, diagonal)
         weighted = current * inverse[None, :]
         second_term = jnp.dot(
-            scaled_gram, first_iter, precision=high, preferred_element_type=jnp.float32
+            scaled_gram, first_iter, precision=fast, preferred_element_type=jnp.float32
         )
         middle = 3.0 * identity - jnp.dot(
-            first_iter, second_term, precision=high, preferred_element_type=jnp.float32
+            first_iter, second_term, precision=fast, preferred_element_type=jnp.float32
         )
-        product = jnp.dot(weighted, middle, precision=high, preferred_element_type=jnp.float32)
+        product = jnp.dot(weighted, middle, precision=fast, preferred_element_type=jnp.float32)
         current = (
-            jnp.dot(product, first_iter, precision=high, preferred_element_type=jnp.float32)
+            jnp.dot(product, first_iter, precision=fast, preferred_element_type=jnp.float32)
             * factor[None, :]
         )
         upper = current[:, :BLK]

time: 473 us -> 387 us (0.82)
  matrix products: 113 us -> 68.1 us
  local copies, waits for them, and re-layouts: 50 us -> 17.8 us
  other arithmetic: 25.7 us -> 17.4 us
    dot_general x8, matrix products: 95.1 us -> 51 us  [the longest x2 20.8 us: per_device(): jnp.dot(scaled_gram, first_iter, precision=fast, preferred_element_type=j...]
    gather x2 -> x0, local copies, waits for them, and re-layouts: 34.2 us -> none  [normalize(): diagonal = jnp.diagonal(gram) + epsilon]
    concatenate x4 -> x0, other arithmetic: 11.4 us -> none  [the longest x2 8.32 us: per_device(): jnp.concatenate([jnp.concatenate([upper_gram, cross_gram], axis=1), jnp.c...]
where the time goes in v1:
time: 387 us; the launch traced here: 380 us
  waiting for transfers between devices  210 us (54%)
  matrix products  68.1 us (18%)
  blocking collectives  34.5 us (9%)
  local copies, waits for them, and re-layouts  17.8 us (5%)
  other arithmetic  17.4 us (4%)
  starting transfers between devices  16.5 us (4%)
  between operations  15.6 us (4%)
    psum x2, waiting for transfers between devices, per_device(): lax.psum((inner_gram(upper, upper), inner_gram(lower, lower), inner_gram(...  174 us
    ppermute x4, waiting for transfers between devices, from_behind(): return lax.ppermute(x, axis, pairs)  35.5 us
    all_to_all x1, blocking collectives, per_device(): lax.all_to_all(slots, 'pair', split_axis=1, concat_axis=0, tiled=True)  34.5 us
    dot_general x2, matrix products, per_device(): jnp.dot(scaled_gram, first_iter, precision=fast, preferred_element_type=j...  20.8 us
    dot_general x6, matrix products, inner_gram(): lax.dot_general(left, right, (((0,), (0,)), ((), ())), precision=high, pr...  17 us
    ppermute x4, starting transfers between devices, from_behind(): return lax.ppermute(x, axis, pairs)  16.2 us
    dot_general x2, matrix products, per_device(): jnp.dot(first_iter, second_term, precision=fast, preferred_element_type=j...  14.8 us
    dot_general x2, matrix products, per_device(): jnp.dot(product, first_iter, precision=fast, preferred_element_type=jnp.f...  8.15 us
  transfers between devices with their start and end apart: 6, of which 6 were waited for; matrix products, arithmetic and copies ran while one was open for 0% of the time, Pallas kernels for 0%

profile of v1, /device:TPU:97, one launch (start us, length us, event | category | flops | bytes accessed | tf_op | source)
XLA Modules:
  0.0 379.6 jit_solution(4020114131448537203)
XLA Ops:
  6.5 0.7 compare_and_fusion
  7.2 0.7 compare_select_fusion
  7.9 0.1 broadcast_in_dim.33
  8.1 3.2 copy.25
  11.2 2.3 gather_fusion
  13.5 2.5 copy.16
  16.0 1.9 gather.7
  18.0 0.2 broadcast_select_fusion
  18.2 1.2 copy.17
  19.5 34.5 %all_to_all.16 = f32[32,16,1024]{2,0,1:T(8,128)S(1)} all-to-all(f32[32,16,1024]{2,0,1:T(8,128)S(1)} %copy.17), channel_id=1, replica_groups=mesh['pair'=16,'rows'=8] {'pair'}, dimensions={1} | all-to-all | bytes 4194304 | tf_op jit(solution)/shard_map/all_to_all | solution.py:50
  53.9 2.9 fusion.51
  56.8 2.8 fusion.53
  59.6 2.8 fusion.56
  62.5 0.3 all-reduce.5.cloned.1.call-start
  62.8 87.7 %all-reduce.7.cloned.1.call-done = (f32[512,512]{1,0:T(8,128)}, f32[512,512]{1,0:T(8,128)}, f32[512,512]{0,1:T(8,128)}) async-done(((f32[512,512]{1,0:T(8,128)}, f32[512,512]{1,0:T(8,128)}, f32[512,512]{0,1:T(8,128)}), (f32[512,512]{1,0:T(8,128)}, f32[512,512]{1,0:T(8,128)}, f32[512,512]{0,1:T(8,128)})) %all-reduce.7.cloned.1.call-update) | async-done | bytes 3145744 | tf_op jit(solution)/shard_map/psum | solution.py:56
  150.5 2.6 copy.19
  153.1 1.6 select_reduce_fusion.2
  154.7 3.7 multiply_reduce_fusion.1
  159.2 10.3 %fusion.16 = f32[1024,1024]{1,0:T(8,128)S(1)} fusion(f32[]{:T(128)S(6)} %div.44, f32[1024]{0:T(1024)S(1)} %fusion.59, f32[512,512]{1,0:T(8,128)S(1)} %copy-done.1, f32[512,512]{1,0:T(8,128)} %bitcast.29, f32[512,512]{1,0:T(8,128)} %copy.19, f32[512,512]{1,0:T(8,128)} %get-tuple-element.9), kind=kOutput, calls=%fused_computation.21 | convolution fusion | flops 6459228160 | bytes 8392708 | tf_op jit(solution)/shard_map/dot_general | solution.py:69
  169.5 7.6 %fusion.14 = f32[1024,1024]{1,0:T(8,128)S(1)} fusion(f32[1024,1024]{1,0:T(8,128)S(1)} %fusion.16, f32[]{:T(128)S(6)} %div.44, f32[1024]{0:T(1024)S(1)} %fusion.59, f32[512,512]{1,0:T(8,128)S(1)} %copy-done.1, f32[512,512]{1,0:T(8,128)S(1)} %bitcast.30, f32[512,512]{1,0:T(8,128)S(1)} %copy-done.7, f32[512,512]{1,0:T(8,128)S(1)} %copy-done.2), kind=kOutput, calls=%fused_computation.20 | convolution fusion | flops 6452936704 | bytes 12587012 | tf_op jit(solution)/shard_map/dot_general | solution.py:72
  177.1 3.7 fusion.1
  180.8 4.0 %fusion.43 = f32[512,1024]{1,0:T(8,128)S(1)} fusion(f32[512,1024]{1,0:T(8,128)S(1)} %fusion.1, f32[1024]{0:T(1024)S(1)} %multiply_divide_fusion.1, f32[]{:T(128)S(6)} %div.44, f32[1024]{0:T(1024)S(1)} %fusion.59, f32[512,512]{1,0:T(8,128)S(1)} %copy-done.1, f32[512,512]{1,0:T(8,128)S(1)} %bitcast.31, f32[512,512]{1,0:T(8,128)S(1)} %copy-done.7, ...), kind=kOutput, calls=%fused_computation.52 | convolution fusion | flops 3232235520 | bytes 8396804 | tf_op jit(solution)/shard_map/dot_general | solution.py:77
  184.8 1.3 copy-done
  186.1 0.2 slice_select_fusion.5
  186.3 6.1 %collective-permute-start = (f32[512,512]{1,0:T(8,128)S(1)}, f32[512,512]{1,0:T(8,128)S(1)}, u32[]{:S(2)}, u32[]{:S(2)}) collective-permute-start(f32[512,512]{1,0:T(8,128)S(1)} %get-tuple-element.17), channel_id=1, source_target_pairs={{0,8},{8,16},{16,24},{24,32},{32,40},{40,48},{48,56},{56,64},{64,7... | collective-permute-start | bytes 3145736 | tf_op jit(solution)/shard_map/ppermute | solution.py:18
  192.4 2.1 collective-permute-start.1
  194.5 9.6 %collective-permute-done = f32[512,512]{1,0:T(8,128)S(1)} collective-permute-done((f32[512,512]{1,0:T(8,128)S(1)}, f32[512,512]{1,0:T(8,128)S(1)}, u32[]{:S(2)}, u32[]{:S(2)}) %collective-permute-start) | collective-permute-done | bytes 1048608 | tf_op jit(solution)/shard_map/ppermute | solution.py:18
  204.1 8.1 %collective-permute-done.1 = f32[512,512]{1,0:T(8,128)} collective-permute-done((f32[512,512]{1,0:T(8,128)S(1)}, f32[512,512]{1,0:T(8,128)}, u32[]{:S(2)}, u32[]{:S(2)}) %collective-permute-start.1) | collective-permute-done | bytes 1048608 | tf_op jit(solution)/shard_map/ppermute | solution.py:18
  212.2 1.9 slice_select_fusion.4
  214.1 2.8 fusion.83
  217.0 2.8 fusion.85
  219.8 2.8 fusion.84
  222.7 86.5 %all-reduce.5.cloned.1.call-done = (f32[512,512]{1,0:T(8,128)}, f32[512,512]{1,0:T(8,128)}, f32[512,512]{1,0:T(8,128)}) async-done(((f32[512,512]{1,0:T(8,128)}, f32[512,512]{1,0:T(8,128)}, f32[512,512]{1,0:T(8,128)}), (f32[512,512]{1,0:T(8,128)}, f32[512,512]{1,0:T(8,128)}, f32[512,512]{1,0:T(8,128)})) %all-reduce.5.cloned.1.call-update) | async-done | bytes 3145744 | tf_op jit(solution)/shard_map/psum | solution.py:56
  309.2 1.4 select_reduce_fusion
  310.5 1.3 select_reduce_fusion.1
  311.8 2.5 copy.20
  314.4 3.7 multiply_reduce_fusion
  318.8 10.5 %fusion.10 = f32[1024,1024]{1,0:T(8,128)S(1)} fusion(f32[]{:T(128)S(6)} %div.49, f32[1024]{0:T(1024)S(1)} %fusion.58, f32[512,512]{1,0:T(8,128)S(1)} %copy-done.4, f32[512,512]{1,0:T(8,128)} %copy.20, f32[512,512]{1,0:T(8,128)} %get-tuple-element.7, f32[512,512]{1,0:T(8,128)} %get-tuple-element.6), kind=kOutput, calls=%fused_computation.18 | convolution fusion | flops 6459228160 | bytes 8392708 | tf_op jit(solution)/shard_map/dot_general | solution.py:69
  329.3 7.2 %fusion.8 = f32[1024,1024]{1,0:T(8,128)S(1)} fusion(f32[1024,1024]{1,0:T(8,128)S(1)} %fusion.10, f32[]{:T(128)S(6)} %div.49, f32[1024]{0:T(1024)S(1)} %fusion.58, f32[512,512]{1,0:T(8,128)S(1)} %copy-done.4, f32[512,512]{1,0:T(8,128)S(1)} %copy-done.8, f32[512,512]{1,0:T(8,128)S(1)} %copy-done.6, f32[512,512]{1,0:T(8,128)S(1)} %copy-done.5), kind=kOutput, calls=%fused_computation.17 | convolution fusion | flops 6452936704 | bytes 12587012 | tf_op jit(solution)/shard_map/dot_general | solution.py:72
  336.5 3.7 fusion.3
  340.2 4.2 %fusion.46 = f32[512,1024]{1,0:T(8,128)S(1)} fusion(f32[512,1024]{1,0:T(8,128)S(1)} %fusion.3, f32[1024]{0:T(1024)S(1)} %multiply_divide_fusion, f32[]{:T(128)S(6)} %div.49, f32[1024]{0:T(1024)S(1)} %fusion.58, f32[512,512]{1,0:T(8,128)S(1)} %copy-done.4, f32[512,512]{1,0:T(8,128)S(1)} %copy-done.8, f32[512,512]{1,0:T(8,128)S(1)} %copy-done.6, ...), kind=kOutput, calls=%fused_computation.53 | convolution fusion | flops 3232235520 | bytes 8396804 | tf_op jit(solution)/shard_map/dot_general | solution.py:77
  344.4 0.2 slice_select_fusion.2
  344.7 6.1 %collective-permute-start.2 = (f32[512,512]{1,0:T(8,128)S(1)}, f32[512,512]{1,0:T(8,128)S(1)}, u32[]{:S(2)}, u32[]{:S(2)}) collective-permute-start(f32[512,512]{1,0:T(8,128)S(1)} %get-tuple-element.13), channel_id=1, source_target_pairs={{0,8},{8,16},{16,24},{24,32},{32,40},{40,48},{48,56},{56,64},{64,7... | collective-permute-start | bytes 3145736 | tf_op jit(solution)/shard_map/ppermute | solution.py:18
  350.8 1.9 collective-permute-start.3
  352.7 9.8 %collective-permute-done.2 = f32[512,512]{1,0:T(8,128)S(1)} collective-permute-done((f32[512,512]{1,0:T(8,128)S(1)}, f32[512,512]{1,0:T(8,128)S(1)}, u32[]{:S(2)}, u32[]{:S(2)}) %collective-permute-start.2) | collective-permute-done | bytes 1048608 | tf_op jit(solution)/shard_map/ppermute | solution.py:18
  362.5 8.0 %collective-permute-done.3 = f32[512,512]{1,0:T(8,128)S(1)} collective-permute-done((f32[512,512]{1,0:T(8,128)S(1)}, f32[512,512]{1,0:T(8,128)S(1)}, u32[]{:S(2)}, u32[]{:S(2)}) %collective-permute-start.3) | collective-permute-done | bytes 1048608 | tf_op jit(solution)/shard_map/ppermute | solution.py:18
  370.5 0.3 slice_select_fusion.1
  370.9 1.5 pad_maximum_fusion
  (27 shorter events, 0.2 us)
Async XLA Ops:
  6.5 144.0 %all-reduce.7.cloned.1.call-start = ((), (), s32[]{:S(2)}) async-start(), calls=%async_computation.2 | async-start | bytes 6291456 | tf_op jit(solution)/shard_map/psum | solution.py:56
  62.5 246.7 %all-reduce.5.cloned.1.call-start = ((), (), s32[]{:S(2)}) async-start(), calls=%async_computation.1 | async-start | bytes 6291456 | tf_op jit(solution)/shard_map/psum | solution.py:56
  150.5 4.2 %copy-start.1 = (f32[512,512]{1,0:T(8,128)S(1)}, f32[512,512]{1,0:T(8,128)}, u32[]{:S(2)}) copy-start(f32[512,512]{1,0:T(8,128)} %get-tuple-element.8) | copy-start | bytes 3145732
  159.2 10.3 %copy-start.2 = (f32[512,512]{1,0:T(8,128)S(1)}, f32[512,512]{1,0:T(8,128)}, u32[]{:S(2)}) copy-start(f32[512,512]{1,0:T(8,128)} %get-tuple-element.9) | copy-start | bytes 3145732
  159.2 10.3 %copy-start.3 = (f32[512,512]{0,1:T(8,128)S(1)}, f32[512,512]{0,1:T(8,128)}, u32[]{:S(2)}) copy-start(f32[512,512]{0,1:T(8,128)} %get-tuple-element.10) | copy-start | bytes 3145732
  159.2 10.3 %copy-start.7 = (f32[512,512]{1,0:T(8,128)S(1)}, f32[512,512]{1,0:T(8,128)}, u32[]{:S(2)}) copy-start(f32[512,512]{1,0:T(8,128)} %copy.19) | copy-start | bytes 3145732
  184.8 1.3 copy-start
  186.3 17.8 %collective-permute-start = (f32[512,512]{1,0:T(8,128)S(1)}, f32[512,512]{1,0:T(8,128)S(1)}, u32[]{:S(2)}, u32[]{:S(2)}) collective-permute-start(f32[512,512]{1,0:T(8,128)S(1)} %get-tuple-element.17), channel_id=1, source_target_pairs={{0,8},{8,16},{16,24},{24,32},{32,40},{40,48},{48,56},{56,64},{64,7... | collective-permute-start | bytes 3145736 | tf_op jit(solution)/shard_map/ppermute | solution.py:18
  192.4 19.8 %collective-permute-start.1 = (f32[512,512]{1,0:T(8,128)S(1)}, f32[512,512]{1,0:T(8,128)}, u32[]{:S(2)}, u32[]{:S(2)}) collective-permute-start(f32[512,512]{1,0:T(8,128)S(1)} %get-tuple-element.18), channel_id=1, source_target_pairs={{8,0},{16,8},{24,16},{32,24},{40,32},{48,40},{56,48},{64,56},{72,6... | collective-permute-start | bytes 3145736 | tf_op jit(solution)/shard_map/ppermute | solution.py:18
  309.1 5.2 %copy-start.4 = (f32[512,512]{1,0:T(8,128)S(1)}, f32[512,512]{1,0:T(8,128)}, u32[]{:S(2)}) copy-start(f32[512,512]{1,0:T(8,128)} %get-tuple-element.5) | copy-start | bytes 3145732
  318.8 10.6 %copy-start.5 = (f32[512,512]{1,0:T(8,128)S(1)}, f32[512,512]{1,0:T(8,128)}, u32[]{:S(2)}) copy-start(f32[512,512]{1,0:T(8,128)} %get-tuple-element.6) | copy-start | bytes 3145732
  318.8 10.6 %copy-start.6 = (f32[512,512]{1,0:T(8,128)S(1)}, f32[512,512]{1,0:T(8,128)}, u32[]{:S(2)}) copy-start(f32[512,512]{1,0:T(8,128)} %get-tuple-element.7) | copy-start | bytes 3145732
  318.8 10.6 %copy-start.8 = (f32[512,512]{1,0:T(8,128)S(1)}, f32[512,512]{1,0:T(8,128)}, u32[]{:S(2)}) copy-start(f32[512,512]{1,0:T(8,128)} %copy.20) | copy-start | bytes 3145732
  344.7 17.8 %collective-permute-start.2 = (f32[512,512]{1,0:T(8,128)S(1)}, f32[512,512]{1,0:T(8,128)S(1)}, u32[]{:S(2)}, u32[]{:S(2)}) collective-permute-start(f32[512,512]{1,0:T(8,128)S(1)} %get-tuple-element.13), channel_id=1, source_target_pairs={{0,8},{8,16},{16,24},{24,32},{32,40},{40,48},{48,56},{56,64},{64,7... | collective-permute-start | bytes 3145736 | tf_op jit(solution)/shard_map/ppermute | solution.py:18
  350.8 19.7 %collective-permute-start.3 = (f32[512,512]{1,0:T(8,128)S(1)}, f32[512,512]{1,0:T(8,128)S(1)}, u32[]{:S(2)}, u32[]{:S(2)}) collective-permute-start(f32[512,512]{1,0:T(8,128)S(1)} %get-tuple-element.14), channel_id=1, source_target_pairs={{8,0},{16,8},{24,16},{32,24},{40,32},{48,40},{56,48},{64,56},{72,6... | collective-permute-start | bytes 3145736 | tf_op jit(solution)/shard_map/ppermute | solution.py:18
Sparse Core Ops, SparseCore 0:
  62.6 87.8 all-reduce.6
  222.8 86.3 all-reduce.4
